TPU v7x, 512 devices: a whole 4x4x16 slice. The times are simulated.
512 devices in a mesh: gx: 16 (over x, z_hi), gy: 8 (over y, core), gz: 4 (over z_lo).
Axes of the slice: x: 4, y: 4, z: 16 (z_hi: 4, z_lo: 4; z = z_hi * 4 + z_lo), core: 2. Of those that a mesh axis runs over, the one named last changes fastest.
Arguments:
- offsets: float32 [3, 32, 16, 8, 128], P(None, 'gx', 'gy', 'gz'), may hold values from 0 to 1
- velocity: float32 [3, 32, 16, 8, 128], P(None, 'gx', 'gy', 'gz'), may hold values from -3 to 3
- density: float32 [32, 16, 8, 128], P('gx', 'gy', 'gz'), may hold values from 0.98 to 1.02
- mass: float32 [32, 16, 8, 128], P('gx', 'gy', 'gz'), may hold values from 0.008 to 0.024
- occupancy: int32 [32, 16, 8], P('gx', 'gy', 'gz'), may hold values from 32 to 128, as said below
- move_direction: int32 [32, 16, 8, 128], P('gx', 'gy', 'gz'), may hold values from 0 to 2, as said below
- move_slot: int32 [32, 16, 8, 128], P('gx', 'gy', 'gz'), may hold values from 0 to 127, as said below
Outputs:
- position_next: float32 [3, 32, 16, 8, 128], P(None, 'gx', 'gy', 'gz')
- velocity_next: float32 [3, 32, 16, 8, 128], P(None, 'gx', 'gy', 'gz')
- density_next: float32 [32, 16, 8, 128], P('gx', 'gy', 'gz')
- arrivals: float32 [7, 2, 16, 8, 4, 128], P(None, None, 'gx', 'gy', 'gz')
Inputs may be any that keep to these rules, and one draw needn't show every extreme that they name: Slots 0 to occupancy - 1 of a cell are live; some cell has all 128 slots live. `move_direction`: 0 on every slot that is not live. `move_slot`: among the live particles of one device with the same nonzero move_direction the slots are distinct, so at most 128 leave a device in one direction; some device sends exactly 128 in one direction. 0 where move_direction is 0.
All inputs are finite; a program needn't handle non-finite values.
Results may differ from a plain program's by a relative error of at most 0.0003.
Values sent between devices are 32-bit elements; how exact they have to be, the bound alone decides.
A program may use at most 64 MiB of HBM per device.

v0:
```python
import math

import jax
import jax.numpy as jnp
from jax import lax
from jax.experimental import pallas as pl
from jax.experimental.pallas import tpu as pltpu
from jax.sharding import PartitionSpec as P

F32 = jnp.float32
BF16 = jnp.bfloat16
MESH = pl.DeviceIdType.MESH
AXES = ("gx", "gy", "gz")
SLOTS = 128

SMOOTH = 0.5
KERNEL_NORM = 21.0 / (16.0 * math.pi * SMOOTH**3)
GRADIENT = 5.0 * KERNEL_NORM / SMOOTH**2
SOUND_SPEED = 10.0
STIFFNESS = SOUND_SPEED**2 / 7.0
TIME_STEP = 0.1
HALF_STEP = 0.05
EPS = 0.01 * SMOOTH * SMOOTH
TINY = 1e-12
CHUNK = 16

REGIONS = [
    (dx, dy, dz)
    for dx in (-1, 0, 1)
    for dy in (-1, 0, 1)
    for dz in (-1, 0, 1)
    if (dx, dy, dz) != (0, 0, 0)
]
SLOT_OF = {region: at for at, region in enumerate(REGIONS)}


def split3(value):
    first = value.astype(BF16).astype(F32)
    rest = value - first
    second = rest.astype(BF16).astype(F32)
    return first, second, rest - second


def row_iota():
    return lax.broadcasted_iota(jnp.int32, (8, SLOTS), 0)


def kernel(
    off_ref, vel_ref, rho_ref, mass_ref, occ_ref, dir_ref, slot_ref,
    pos_out, vel_out, rho_out, arr_out,
    first, half, near_feat, own_feat, near_rows, own_q, own_t, geo, acc, code, fresh, lists, landed,
    send_sem, recv_sem, list_send, list_recv,
):
    place = [lax.axis_index(axis) for axis in AXES]
    count = [lax.axis_size(axis) for axis in AXES]
    row = row_iota()
    lane = lax.broadcasted_iota(jnp.int32, (8, SLOTS), 1)

    first[...] = jnp.zeros_like(first)
    half[...] = jnp.zeros_like(half)
    landed[...] = jnp.zeros_like(landed)

    barrier = pltpu.get_barrier_semaphore()
    greeted = jnp.int32(0)
    for at, axis in enumerate(AXES):
        for step in (-1, 1):
            other = place[at] + step
            there = jnp.logical_and(other >= 0, other < count[at])

            @pl.when(there)
            def _():
                pl.semaphore_signal(barrier, inc=1, device_id={axis: other}, device_id_type=MESH)

            greeted = greeted + there.astype(jnp.int32)

    def halo_copy(phase, region):
        at = max(k for k in range(3) if region[k] != 0)
        buffer = (first, half)[phase]
        source, target = [], []
        for k in range(3):
            span = {-1: 0, 0: pl.ds(1, 2), 1: 3}[region[k]]
            target.append(span)
            source.append({-1: 2, 1: 1}[region[k]] if k == at else span)
        other = lax.rem(place[at] - region[at] + count[at], count[at])
        copy = pltpu.make_async_remote_copy(
            src_ref=buffer.at[tuple(source)],
            dst_ref=buffer.at[tuple(target)],
            send_sem=send_sem.at[phase, SLOT_OF[region]],
            recv_sem=recv_sem.at[phase, SLOT_OF[region]],
            device_id={AXES[at]: other},
            device_id_type=MESH,
        )
        sends = place[at] < count[at] - 1 if region[at] < 0 else place[at] > 0
        receives = place[at] > 0 if region[at] < 0 else place[at] < count[at] - 1
        return copy, sends, receives

    def start(phase, regions):
        for region in regions:
            copy, sends, _ = halo_copy(phase, region)

            @pl.when(sends)
            def _():
                copy.start()

    def wait_in(phase, regions):
        for region in regions:
            copy, _, receives = halo_copy(phase, region)

            @pl.when(receives)
            def _():
                copy.wait_recv()

    def wait_out(phase, regions):
        for region in regions:
            copy, sends, _ = halo_copy(phase, region)

            @pl.when(sends)
            def _():
                copy.wait_send()

    def cell_tile(phase, cx, cy, cz):
        tile = first[cx, cy, cz]
        if phase == 0:
            return tile
        now = half[cx, cy, cz]
        return jnp.concatenate([tile[0:3] + HALF_STEP * tile[3:6], now, tile[7:8]], 0)

    def features(phase, cx, cy, cz, own=None):
        tile = cell_tile(phase, cx, cy, cz)
        shift = jnp.where(row == 0, cx, jnp.where(row == 1, cy, jnp.where(row == 2, cz, 2))) - 2
        moved = tile + shift.astype(F32)
        x, v, rho, m = moved[0:3], moved[3:6], moved[6:7], moved[7:8]
        norm = jnp.sum(x * x, axis=0, keepdims=True)
        cross = jnp.sum(x * v, axis=0, keepdims=True)
        parts = split3(jnp.concatenate([x, v, norm, cross], 0))
        zero = jnp.zeros((8, SLOTS), F32)
        dist, along = [], []
        for at, part in enumerate(parts):
            one = 1.0 if at == 0 else 0.0
            dist.append(jnp.where(row < 3, -2.0 * part, jnp.where(row == 6, one, 0.0)))
            swapped = jnp.concatenate([part[3:6], part[0:3], part[6:8]], 0)
            along.append(jnp.where(row < 6, -swapped, jnp.where(row == 7, one, 0.0)))
        pad = jnp.zeros((5, SLOTS), F32)
        dist_own = jnp.concatenate([part[6:7] for part in parts] + [pad], 0)
        along_own = jnp.concatenate([part[7:8] for part in parts] + [pad], 0)
        cell = cx * 16 + cy * 4 + cz
        for at, (blocks, last) in enumerate(((dist, dist_own), (along, along_own))):
            full = jnp.concatenate(
                [blocks[0], blocks[1], blocks[2], blocks[0], blocks[1], blocks[0], last, zero], 0
            )
            near_feat[cell, :, at * SLOTS : (at + 1) * SLOTS] = full.astype(BF16)
        q = jnp.where(m > 0, rho, 1.0)
        q2 = q * q
        term = STIFFNESS * (q2 * q2 * q2 * q - 1.0) / q2
        near_rows[cell] = jnp.concatenate([x, q, term, m, zero[0:2]], 0)
        if own is not None:
            a, b, c = parts
            ones = jnp.where(row < 3, 1.0, 0.0)
            extra = jnp.concatenate([q, term, zero[0:6]], 0)
            stack = jnp.concatenate([a, a, a, b, b, c, ones, extra], 0).T
            own_feat[own] = stack.astype(BF16)
            rows = pl.ds(pl.multiple_of(own * SLOTS, SLOTS), SLOTS)
            own_q[rows, :] = jnp.broadcast_to(stack[:, 56:57], (SLOTS, SLOTS))
            own_t[rows, :] = jnp.broadcast_to(stack[:, 57:58], (SLOTS, SLOTS))

    def geometry(slot, owns, nears):
        left = jnp.concatenate([own_feat[o] for o in owns], 0) if len(owns) > 1 else own_feat[owns[0]]
        for k, near in enumerate(nears):
            geo[slot, k, 0 : len(owns) * SLOTS, :] = jnp.dot(
                left, near_feat[near], preferred_element_type=F32
            )

    def pairs(slot, owns, nears):
        rows = []
        for near in nears:
            tile = near_rows[near]
            rows.append([jnp.broadcast_to(tile[t : t + 1], (CHUNK, SLOTS)) for t in range(6)])
        for at, o in enumerate(owns):
            for piece in range(0, SLOTS, CHUNK):
                where = pl.ds(pl.multiple_of(o * SLOTS, SLOTS) + piece, CHUNK)
                here = slice(at * SLOTS + piece, at * SLOTS + piece + CHUNK)
                own_qs, own_ts = own_q[where, :], own_t[where, :]
                sums = [acc[t, where, :] for t in range(5)]
                for k in range(len(nears)):
                    x0, x1, x2, q, term, m = rows[k]
                    dist_sq = jnp.maximum(geo[slot, k, here, 0:SLOTS], TINY)
                    along = geo[slot, k, here, SLOTS : 2 * SLOTS]
                    fall = jnp.maximum(1.0 - dist_sq * lax.rsqrt(dist_sq), 0.0)
                    weight = fall * fall * fall * m
                    closing = jnp.minimum(along, 0.0) / ((dist_sq + EPS) * (own_qs + q))
                    push = weight * ((own_ts + term) - closing)
                    sums[0] = sums[0] + push
                    sums[1] = sums[1] + push * x0
                    sums[2] = sums[2] + push * x1
                    sums[3] = sums[3] + push * x2
                    sums[4] = sums[4] + weight * along
                for t in range(5):
                    acc[t, where, :] = sums[t]

    def run_class(steps, plan):
        geometry(0, *plan(0))

        def two(at, carry):
            step = 2 * at
            geometry(1, *plan(step + 1))
            pairs(0, *plan(step))
            geometry(0, *plan(jnp.minimum(step + 2, steps - 1)))
            pairs(1, *plan(step + 1))
            return carry

        lax.fori_loop(0, steps // 2, two, 0)

    def cell_at(cx, cy, cz):
        return cx * 16 + cy * 4 + cz

    def own_plan(step):
        pair, side = step // 2, step % 2
        nears = [cell_at(1 + side, 1 + k // 2, 1 + k % 2) for k in range(4)]
        return [2 * pair, 2 * pair + 1], nears

    def face_plan(axis):
        others = [k for k in range(3) if k != axis]

        def plan(step):
            side, which = step // 2, step % 2
            owns = []
            for last in range(2):
                spot = [None] * 3
                spot[axis], spot[others[0]], spot[others[1]] = side, which, last
                owns.append(spot[0] * 4 + spot[1] * 2 + spot[2])
            nears = []
            for k in range(4):
                spot = [None] * 3
                spot[axis], spot[others[0]], spot[others[1]] = side * 3, 1 + k // 2, 1 + k % 2
                nears.append(cell_at(*spot))
            return owns, nears

        return plan

    def edge_plan(free):
        others = [k for k in range(3) if k != free]

        def plan(step):
            sides = (step // 2, step % 2)
            owns, nears = [], []
            for last in range(2):
                spot = [None] * 3
                spot[others[0]], spot[others[1]], spot[free] = sides[0], sides[1], last
                owns.append(spot[0] * 4 + spot[1] * 2 + spot[2])
                spot[others[0]], spot[others[1]], spot[free] = sides[0] * 3, sides[1] * 3, 1 + last
                nears.append(cell_at(*spot))
            return owns, nears

        return plan

    def corner_plan(step):
        x, y, z = step // 4, (step // 2) % 2, step % 2
        return [step], [cell_at(3 * x, 3 * y, 3 * z)]

    def build(phase, total, spot_of):
        def one(at, carry):
            features(phase, *spot_of(at))
            return carry

        lax.fori_loop(0, total, one, 0)

    def face_spot(axis):
        others = [k for k in range(3) if k != axis]

        def spot(at):
            out = [None] * 3
            out[axis] = (at // 4) * 3
            out[others[0]], out[others[1]] = 1 + (at // 2) % 2, 1 + at % 2
            return out

        return spot

    def edge_spot(free):
        others = [k for k in range(3) if k != free]

        def spot(at):
            out = [None] * 3
            out[others[0]], out[others[1]], out[free] = (at // 4) * 3, ((at // 2) % 2) * 3, 1 + at % 2
            return out

        return spot

    def corner_spot(at):
        return [(at // 4) * 3, ((at // 2) % 2) * 3, (at % 2) * 3]

    def build_own(phase):
        def one(at, carry):
            features(phase, 1 + at // 4, 1 + (at // 2) % 2, 1 + at % 2, own=at)
            return carry

        lax.fori_loop(0, 8, one, 0)

    x_faces = [(-1, 0, 0), (1, 0, 0)]
    y_faces = [(0, -1, 0), (0, 1, 0)]
    z_faces = [(0, 0, -1), (0, 0, 1)]
    xy_edges = [r for r in REGIONS if r[0] and r[1] and not r[2]]
    xz_edges = [r for r in REGIONS if r[0] and not r[1] and r[2]]
    yz_edges = [r for r in REGIONS if not r[0] and r[1] and r[2]]
    corners = [r for r in REGIONS if r[0] and r[1] and r[2]]

    def rates(phase):
        acc[...] = jnp.zeros_like(acc)
        build_own(phase)
        run_class(8, own_plan)
        wait_in(phase, y_faces)
        start(phase, yz_edges)
        build(phase, 8, face_spot(1))
        run_class(4, face_plan(1))
        wait_in(phase, x_faces)
        start(phase, xy_edges + xz_edges)
        wait_in(phase, z_faces)
        build(phase, 8, face_spot(2))
        run_class(4, face_plan(2))
        build(phase, 8, face_spot(0))
        run_class(4, face_plan(0))
        wait_in(phase, xy_edges)
        start(phase, corners)
        wait_in(phase, yz_edges)
        build(phase, 8, edge_spot(0))
        run_class(4, edge_plan(0))
        build(phase, 8, edge_spot(2))
        run_class(4, edge_plan(2))
        wait_in(phase, xz_edges)
        build(phase, 8, edge_spot(1))
        run_class(4, edge_plan(1))
        wait_in(phase, corners)
        build(phase, 8, corner_spot)
        run_class(8, corner_plan)

    def own_rates(o, cx, cy, cz):
        rows = pl.ds(pl.multiple_of(o * SLOTS, SLOTS), SLOTS)
        column = lax.broadcasted_iota(jnp.int32, (SLOTS, SLOTS), 1)
        table = jnp.zeros((SLOTS, SLOTS), F32)
        for t in range(5):
            table = jnp.where(column == t, jnp.sum(acc[t, rows, :], axis=1, keepdims=True), table)
        sums = table.T[0:8]
        x = near_rows[cell_at(cx, cy, cz)][0:3]
        gravity = jnp.where(row == 2, 1.0, 0.0)[0:3]
        accel = GRADIENT * (x * sums[0:1] - sums[1:4]) - gravity
        return accel, -GRADIENT * sums[4:5]

    filled = jnp.zeros((8, SLOTS), jnp.int32)
    for o in range(8):
        filled = jnp.where(row == o, occ_ref[o], filled)
    live = lane < filled
    carried = jnp.where(live, mass_ref[...], 0.0)
    for which in (1, 2):
        chosen = jnp.logical_and(live, dir_ref[...] == which)
        code[which - 1] = jnp.where(chosen, slot_ref[...], -1)
    code[2] = jnp.where(jnp.logical_and(live, dir_ref[...] == 0), 1, 0)
    for o in range(8):
        cx, cy, cz = 1 + o // 4, 1 + (o // 2) % 2, 1 + o % 2
        first[cx, cy, cz] = jnp.concatenate(
            [off_ref[k, o : o + 1] for k in range(3)]
            + [vel_ref[k, o : o + 1] for k in range(3)]
            + [rho_ref[o : o + 1], carried[o : o + 1]],
            0,
        )

    pl.semaphore_wait(barrier, greeted)
    start(0, x_faces + y_faces + z_faces)
    rates(0)

    def to_half(o, carry):
        cx, cy, cz = 1 + o // 4, 1 + (o // 2) % 2, 1 + o % 2
        accel, rate = own_rates(o, cx, cy, cz)
        tile = first[cx, cy, cz]
        half[cx, cy, cz] = jnp.concatenate(
            [tile[3:6] + HALF_STEP * accel, tile[6:7] + HALF_STEP * rate], 0
        )
        return carry

    lax.fori_loop(0, 8, to_half, 0)
    start(1, x_faces + y_faces + z_faces)
    rates(1)

    slots = lax.broadcasted_iota(jnp.int32, (SLOTS, SLOTS), 0)

    def to_new(o, found):
        cx, cy, cz = 1 + o // 4, 1 + (o // 2) % 2, 1 + o % 2
        accel, rate = own_rates(o, cx, cy, cz)
        tile = first[cx, cy, cz]
        new_pos = tile[0:3] + TIME_STEP * half[cx, cy, cz][0:3]
        new_vel = tile[3:6] + TIME_STEP * accel
        new_rho = tile[6:7] + TIME_STEP * rate
        new = jnp.concatenate([new_pos, new_vel, new_rho, jnp.zeros((1, SLOTS), F32)], 0)
        stays = jnp.broadcast_to(code[2, pl.ds(o, 1), :], (8, SLOTS)) > 0
        fresh[o] = jnp.where(stays, new, 0.0)
        spot = jnp.where(row == 0, cx - 1, jnp.where(row == 1, cy - 1, jnp.where(row == 2, cz - 1, 0)))
        record = new + spot.astype(F32)
        out = []
        for which, by in ((0, -2.0), (1, 2.0)):
            parts = split3(record + jnp.where(row == 0, by, 0.0))
            left = jnp.concatenate(parts, 0).astype(BF16)
            target = jnp.broadcast_to(code[which, pl.ds(o, 1), :], (SLOTS, SLOTS))
            chosen = jnp.where(slots == target, 1.0, 0.0).astype(BF16)
            hit = lax.dot_general(
                left, chosen, (((1,), (1,)), ((), ())), preferred_element_type=F32
            )
            out.append(found[which] + hit)
        return tuple(out)

    empty = jnp.zeros((24, SLOTS), F32)
    found = lax.fori_loop(0, 8, to_new, (empty, empty))
    for which in range(2):
        lists[which] = (found[which][0:8] + found[which][8:16]) + found[which][16:24]

    def list_copy(which):
        step = 1 if which == 0 else -1
        other = lax.rem(place[0] + step + count[0], count[0])
        copy = pltpu.make_async_remote_copy(
            src_ref=lists.at[which],
            dst_ref=landed.at[which],
            send_sem=list_send.at[which],
            recv_sem=list_recv.at[which],
            device_id={"gx": other},
            device_id_type=MESH,
        )
        upper, lower = place[0] < count[0] - 1, place[0] > 0
        return copy, (upper, lower)[which], (lower, upper)[which]

    for which in range(2):
        copy, sends, _ = list_copy(which)

        @pl.when(sends)
        def _():
            copy.start()

    for o in range(8):
        tile = fresh[o]
        for k in range(3):
            pos_out[k, o : o + 1, :] = tile[k : k + 1]
            vel_out[k, o : o + 1, :] = tile[3 + k : 4 + k]
        rho_out[o : o + 1, :] = tile[6:7]
    wait_out(0, REGIONS)
    wait_out(1, REGIONS)
    for which in range(2):
        copy, sends, receives = list_copy(which)

        @pl.when(receives)
        def _():
            copy.wait_recv()

        @pl.when(sends)
        def _():
            copy.wait_send()

    for which in range(2):
        tile = landed[which]
        for k in range(7):
            arr_out[2 * k + which : 2 * k + which + 1, :] = tile[k : k + 1]


def body(offsets, velocity, density, mass, occupancy, move_direction, move_slot):
    vmem = pl.BlockSpec(memory_space=pltpu.VMEM)
    smem = pl.BlockSpec(memory_space=pltpu.SMEM)
    pos, vel, rho, arr = pl.pallas_call(
        kernel,
        out_shape=(
            jax.ShapeDtypeStruct((3, 8, SLOTS), F32),
            jax.ShapeDtypeStruct((3, 8, SLOTS), F32),
            jax.ShapeDtypeStruct((8, SLOTS), F32),
            jax.ShapeDtypeStruct((14, SLOTS), F32),
        ),
        in_specs=[vmem, vmem, vmem, vmem, smem, vmem, vmem],
        out_specs=(vmem, vmem, vmem, vmem),
        scratch_shapes=[
            pltpu.VMEM((4, 4, 4, 8, SLOTS), F32),
            pltpu.VMEM((4, 4, 4, 4, SLOTS), F32),
            pltpu.VMEM((64, 64, 2 * SLOTS), BF16),
            pltpu.VMEM((8, SLOTS, 64), BF16),
            pltpu.VMEM((64, 8, SLOTS), F32),
            pltpu.VMEM((8 * SLOTS, SLOTS), F32),
            pltpu.VMEM((8 * SLOTS, SLOTS), F32),
            pltpu.VMEM((2, 4, 2 * SLOTS, 2 * SLOTS), F32),
            pltpu.VMEM((5, 8 * SLOTS, SLOTS), F32),
            pltpu.VMEM((3, 8, SLOTS), jnp.int32),
            pltpu.VMEM((8, 8, SLOTS), F32),
            pltpu.VMEM((2, 8, SLOTS), F32),
            pltpu.VMEM((2, 8, SLOTS), F32),
            pltpu.SemaphoreType.DMA((2, 26)),
            pltpu.SemaphoreType.DMA((2, 26)),
            pltpu.SemaphoreType.DMA((2,)),
            pltpu.SemaphoreType.DMA((2,)),
        ],
        compiler_params=pltpu.CompilerParams(
            collective_id=0, has_side_effects=True, vmem_limit_bytes=48 << 20
        ),
        name="sph_step",
    )(
        offsets.reshape(3, 8, SLOTS),
        velocity.reshape(3, 8, SLOTS),
        density.reshape(8, SLOTS),
        mass.reshape(8, SLOTS),
        occupancy.reshape(8),
        move_direction.reshape(8, SLOTS),
        move_slot.reshape(8, SLOTS),
    )
    return (
        pos.reshape(offsets.shape),
        vel.reshape(velocity.shape),
        rho.reshape(density.shape),
        arr.reshape(7, 2, 1, 1, 1, SLOTS),
    )


def solution(mesh):
    placed = (
        P(None, "gx", "gy", "gz", None),
        P(None, "gx", "gy", "gz", None),
        P("gx", "gy", "gz", None),
        P("gx", "gy", "gz", None),
        P("gx", "gy", "gz"),
        P("gx", "gy", "gz", None),
        P("gx", "gy", "gz", None),
    )
    return jax.shard_map(
        body,
        mesh=mesh,
        in_specs=placed,
        out_specs=(
            P(None, "gx", "gy", "gz", None),
            P(None, "gx", "gy", "gz", None),
            P("gx", "gy", "gz", None),
            P(None, None, "gx", "gy", "gz", None),
        ),
        check_vma=False,
    )
```

profile of v0, /device:TPU:1, one launch (start us, length us, event | category | flops | bytes accessed | tf_op | source)
XLA Modules:
  0.0 73.8 jit_solution(17097660262366557189)
XLA Ops:
  0.6 0.0 copy-start
  0.6 0.8 %reshape.45.occ_ref = s32[8]{0:T(128)S(1)} reshape(s32[2,2,2]{2,1,0:T(2,128)} %param.11) | data formatting | bytes 64 | tf_op jit(solution)/shard_map/reshape | solution.py:500
  1.4 0.0 copy-done
  1.4 0.0 copy-start.1
  1.4 0.7 copy-done.1
  2.1 0.0 copy-start.2
  2.1 0.7 copy-done.2
  2.8 0.0 copy-start.3
  2.8 0.7 copy-done.3
  3.5 0.0 copy-start.4
  3.5 0.7 copy-done.4
  4.2 0.0 copy-start.5
  4.2 0.7 copy-done.5
  4.9 66.5 %sph_step.1 = (f32[3,8,128]{2,1,0:T(8,128)S(1)}, f32[3,8,128]{2,1,0:T(8,128)S(1)}, f32[8,128]{1,0:T(8,128)S(1)}, f32[14,128]{1,0:T(8,128)S(1)}) custom-call(f32[3,8,128]{2,1,0:T(8,128)S(1)} %bitcast.12, f32[3,8,128]{2,1,0:T(8,128)S(1)} %bitcast.13, f32[8,128]{1,0:T(8,128)S(1)} %bitcast.15, f32[8,128]{1,0:T(8,128)S(1)} %bitcast.16, s32[8]{0:T(128)S(1)} %reshape.45.occ_ref, ...), custom_call_target="tpu_custom_call" | custom-call | tf_op jit(solution)/shard_map/sph_step/pallas_call | solution.py:462
  71.4 0.6 reshape.51
  72.0 0.6 copy.15
  72.6 0.6 copy.16
  73.2 0.6 copy.17
Async XLA Ops:
  0.6 0.8 %copy-start = (f32[3,2,2,2,128]{4,3,2,1,0:T(2,128)S(1)}, f32[3,2,2,2,128]{4,3,2,1,0:T(2,128)}, u32[]{:S(2)}) copy-start(f32[3,2,2,2,128]{4,3,2,1,0:T(2,128)} %param.7) | copy-start | bytes 36868
  1.4 0.7 copy-start.1
  2.1 0.7 copy-start.2
  2.8 0.7 copy-start.3
  3.5 0.7 copy-start.4
  4.2 0.7 copy-start.5
where the time goes:
time: 74.7 us; the launch traced here: 73.8 us
  Pallas kernels  66.5 us (89%)
  local copies, waits for them, and re-layouts  6.62 us (9%)
    pallas_call x1, Pallas kernels, body(): pl.pallas_call(kernel, out_shape=(jax.ShapeDtypeStruct((3, 8, SLOTS), F32...  66.5 us
    unnamed x15, local copies, waits for them, and re-layouts  5.25 us

commit v1 on v0

--- a/solution.py
+++ b/solution.py
@@ -46,15 +46,25 @@
 
 
 def kernel(
-    off_ref, vel_ref, rho_ref, mass_ref, occ_ref, dir_ref, slot_ref,
+    off_hbm, vel_hbm, rho_hbm, mass_hbm, occ_ref, dir_hbm, slot_hbm,
     pos_out, vel_out, rho_out, arr_out,
+    off_ref, vel_ref, rho_ref, mass_ref, dir_ref, slot_ref,
     first, half, near_feat, own_feat, near_rows, own_q, own_t, geo, acc, code, fresh, lists, landed,
-    send_sem, recv_sem, list_send, list_recv,
+    records, one_hot, load_sem, send_sem, recv_sem, list_send, list_recv,
 ):
     place = [lax.axis_index(axis) for axis in AXES]
     count = [lax.axis_size(axis) for axis in AXES]
     row = row_iota()
     lane = lax.broadcasted_iota(jnp.int32, (8, SLOTS), 1)
+
+    sources = (off_hbm, vel_hbm, rho_hbm, mass_hbm, dir_hbm, slot_hbm)
+    held = (off_ref, vel_ref, rho_ref, mass_ref, dir_ref, slot_ref)
+    loads = [
+        pltpu.make_async_copy(source, target, load_sem.at[at])
+        for at, (source, target) in enumerate(zip(sources, held))
+    ]
+    for load in loads:
+        load.start()
 
     first[...] = jnp.zeros_like(first)
     half[...] = jnp.zeros_like(half)
@@ -163,49 +173,57 @@
             own_q[rows, :] = jnp.broadcast_to(stack[:, 56:57], (SLOTS, SLOTS))
             own_t[rows, :] = jnp.broadcast_to(stack[:, 57:58], (SLOTS, SLOTS))
 
-    def geometry(slot, owns, nears):
-        left = jnp.concatenate([own_feat[o] for o in owns], 0) if len(owns) > 1 else own_feat[owns[0]]
-        for k, near in enumerate(nears):
-            geo[slot, k, 0 : len(owns) * SLOTS, :] = jnp.dot(
-                left, near_feat[near], preferred_element_type=F32
-            )
-
-    def pairs(slot, owns, nears):
-        rows = []
-        for near in nears:
-            tile = near_rows[near]
-            rows.append([jnp.broadcast_to(tile[t : t + 1], (CHUNK, SLOTS)) for t in range(6)])
-        for at, o in enumerate(owns):
-            for piece in range(0, SLOTS, CHUNK):
-                where = pl.ds(pl.multiple_of(o * SLOTS, SLOTS) + piece, CHUNK)
-                here = slice(at * SLOTS + piece, at * SLOTS + piece + CHUNK)
-                own_qs, own_ts = own_q[where, :], own_t[where, :]
-                sums = [acc[t, where, :] for t in range(5)]
-                for k in range(len(nears)):
-                    x0, x1, x2, q, term, m = rows[k]
-                    dist_sq = jnp.maximum(geo[slot, k, here, 0:SLOTS], TINY)
-                    along = geo[slot, k, here, SLOTS : 2 * SLOTS]
-                    fall = jnp.maximum(1.0 - dist_sq * lax.rsqrt(dist_sq), 0.0)
-                    weight = fall * fall * fall * m
-                    closing = jnp.minimum(along, 0.0) / ((dist_sq + EPS) * (own_qs + q))
-                    push = weight * ((own_ts + term) - closing)
-                    sums[0] = sums[0] + push
-                    sums[1] = sums[1] + push * x0
-                    sums[2] = sums[2] + push * x1
-                    sums[3] = sums[3] + push * x2
-                    sums[4] = sums[4] + weight * along
-                for t in range(5):
-                    acc[t, where, :] = sums[t]
+    def geometry(slot, groups):
+        at = 0
+        for owns, nears in groups:
+            left = own_feat[owns[0]]
+            if len(owns) > 1:
+                left = jnp.concatenate([own_feat[o] for o in owns], 0)
+            for near in nears:
+                geo[slot, at, 0 : len(owns) * SLOTS, :] = jnp.dot(
+                    left, near_feat[near], preferred_element_type=F32
+                )
+                at += 1
+
+    def pairs(slot, groups):
+        base = 0
+        for owns, nears in groups:
+            rows = []
+            for near in nears:
+                tile = near_rows[near]
+                rows.append([jnp.broadcast_to(tile[t : t + 1], (CHUNK, SLOTS)) for t in range(6)])
+            for at, o in enumerate(owns):
+                for piece in range(0, SLOTS, CHUNK):
+                    where = pl.ds(pl.multiple_of(o * SLOTS, SLOTS) + piece, CHUNK)
+                    here = slice(at * SLOTS + piece, at * SLOTS + piece + CHUNK)
+                    own_qs, own_ts = own_q[where, :], own_t[where, :]
+                    sums = [acc[t, where, :] for t in range(5)]
+                    for k in range(len(nears)):
+                        x0, x1, x2, q, term, m = rows[k]
+                        dist_sq = jnp.maximum(geo[slot, base + k, here, 0:SLOTS], TINY)
+                        along = geo[slot, base + k, here, SLOTS : 2 * SLOTS]
+                        fall = jnp.maximum(1.0 - dist_sq * lax.rsqrt(dist_sq), 0.0)
+                        weight = fall * fall * fall * m
+                        closing = jnp.minimum(along, 0.0) / ((dist_sq + EPS) * (own_qs + q))
+                        push = weight * ((own_ts + term) - closing)
+                        sums[0] = sums[0] + push
+                        sums[1] = sums[1] + push * x0
+                        sums[2] = sums[2] + push * x1
+                        sums[3] = sums[3] + push * x2
+                        sums[4] = sums[4] + weight * along
+                    for t in range(5):
+                        acc[t, where, :] = sums[t]
+            base += len(nears)
 
     def run_class(steps, plan):
-        geometry(0, *plan(0))
+        geometry(0, plan(0))
 
         def two(at, carry):
             step = 2 * at
-            geometry(1, *plan(step + 1))
-            pairs(0, *plan(step))
-            geometry(0, *plan(jnp.minimum(step + 2, steps - 1)))
-            pairs(1, *plan(step + 1))
+            geometry(1, plan(step + 1))
+            pairs(0, plan(step))
+            geometry(0, plan(jnp.minimum(step + 2, steps - 1)))
+            pairs(1, plan(step + 1))
             return carry
 
         lax.fori_loop(0, steps // 2, two, 0)
@@ -216,53 +234,60 @@
     def own_plan(step):
         pair, side = step // 2, step % 2
         nears = [cell_at(1 + side, 1 + k // 2, 1 + k % 2) for k in range(4)]
-        return [2 * pair, 2 * pair + 1], nears
-
-    def face_plan(axis):
-        others = [k for k in range(3) if k != axis]
-
-        def plan(step):
-            side, which = step // 2, step % 2
-            owns = []
-            for last in range(2):
-                spot = [None] * 3
-                spot[axis], spot[others[0]], spot[others[1]] = side, which, last
-                owns.append(spot[0] * 4 + spot[1] * 2 + spot[2])
-            nears = []
+        return [([2 * pair, 2 * pair + 1], nears)]
+
+    def pick(axis, values):
+        if isinstance(axis, int):
+            return values[axis]
+        return jnp.where(axis == 0, values[0], jnp.where(axis == 1, values[1], values[2]))
+
+    OWN, NEAR = (4, 2, 1), (16, 4, 1)
+
+    def face_group(axis, side, which):
+        low, high = pick(axis, (1, 0, 0)), pick(axis, (2, 2, 1))
+        owns = [
+            side * pick(axis, OWN) + which * pick(low, OWN) + last * pick(high, OWN) for last in range(2)
+        ]
+        nears = [
+            side * 3 * pick(axis, NEAR) + (1 + k // 2) * pick(low, NEAR) + (1 + k % 2) * pick(high, NEAR)
+            for k in range(4)
+        ]
+        return owns, nears
+
+    def yz_face_plan(step):
+        return [face_group(1 + step // 4, (step // 2) % 2, step % 2)]
+
+    def x_face_plan(step):
+        return [face_group(0, step // 2, step % 2)]
+
+    def edge_plan(step):
+        free, side = step // 2, step % 2
+        low, high = pick(free, (1, 0, 0)), pick(free, (2, 2, 1))
+        groups = []
+        for other in range(2):
+            owns = [
+                side * pick(low, OWN) + other * pick(high, OWN) + last * pick(free, OWN)
+                for last in range(2)
+            ]
+            nears = [
+                side * 3 * pick(low, NEAR) + other * 3 * pick(high, NEAR) + (1 + last) * pick(free, NEAR)
+                for last in range(2)
+            ]
+            groups.append((owns, nears))
+        return groups
+
+    def corner_plan(step):
+        return [
+            ([step * 4 + k], [cell_at(3 * step, 3 * (k // 2), 3 * (k % 2))]) for k in range(4)
+        ]
+
+    def build(phase, total, spot_of):
+        def four(at, carry):
             for k in range(4):
-                spot = [None] * 3
-                spot[axis], spot[others[0]], spot[others[1]] = side * 3, 1 + k // 2, 1 + k % 2
-                nears.append(cell_at(*spot))
-            return owns, nears
-
-        return plan
-
-    def edge_plan(free):
-        others = [k for k in range(3) if k != free]
-
-        def plan(step):
-            sides = (step // 2, step % 2)
-            owns, nears = [], []
-            for last in range(2):
-                spot = [None] * 3
-                spot[others[0]], spot[others[1]], spot[free] = sides[0], sides[1], last
-                owns.append(spot[0] * 4 + spot[1] * 2 + spot[2])
-                spot[others[0]], spot[others[1]], spot[free] = sides[0] * 3, sides[1] * 3, 1 + last
-                nears.append(cell_at(*spot))
-            return owns, nears
-
-        return plan
-
-    def corner_plan(step):
-        x, y, z = step // 4, (step // 2) % 2, step % 2
-        return [step], [cell_at(3 * x, 3 * y, 3 * z)]
-
-    def build(phase, total, spot_of):
-        def one(at, carry):
-            features(phase, *spot_of(at))
+                features(phase, *spot_of(4 * at + k))
             return carry
 
-        lax.fori_loop(0, total, one, 0)
+        lax.fori_loop(0, total // 4, four, 0)
 
     def face_spot(axis):
         others = [k for k in range(3) if k != axis]
@@ -289,11 +314,13 @@
         return [(at // 4) * 3, ((at // 2) % 2) * 3, (at % 2) * 3]
 
     def build_own(phase):
-        def one(at, carry):
-            features(phase, 1 + at // 4, 1 + (at // 2) % 2, 1 + at % 2, own=at)
+        def two(at, carry):
+            for k in range(2):
+                o = 2 * at + k
+                features(phase, 1 + o // 4, 1 + (o // 2) % 2, 1 + o % 2, own=o)
             return carry
 
-        lax.fori_loop(0, 8, one, 0)
+        lax.fori_loop(0, 4, two, 0)
 
     x_faces = [(-1, 0, 0), (1, 0, 0)]
     y_faces = [(0, -1, 0), (0, 1, 0)]
@@ -304,33 +331,28 @@
     corners = [r for r in REGIONS if r[0] and r[1] and r[2]]
 
     def rates(phase):
-        acc[...] = jnp.zeros_like(acc)
-        build_own(phase)
         run_class(8, own_plan)
         wait_in(phase, y_faces)
         start(phase, yz_edges)
         build(phase, 8, face_spot(1))
-        run_class(4, face_plan(1))
+        wait_in(phase, z_faces)
+        build(phase, 8, face_spot(2))
+        run_class(8, yz_face_plan)
         wait_in(phase, x_faces)
         start(phase, xy_edges + xz_edges)
-        wait_in(phase, z_faces)
-        build(phase, 8, face_spot(2))
-        run_class(4, face_plan(2))
         build(phase, 8, face_spot(0))
-        run_class(4, face_plan(0))
+        run_class(4, x_face_plan)
         wait_in(phase, xy_edges)
         start(phase, corners)
         wait_in(phase, yz_edges)
         build(phase, 8, edge_spot(0))
-        run_class(4, edge_plan(0))
         build(phase, 8, edge_spot(2))
-        run_class(4, edge_plan(2))
         wait_in(phase, xz_edges)
         build(phase, 8, edge_spot(1))
-        run_class(4, edge_plan(1))
+        run_class(6, edge_plan)
         wait_in(phase, corners)
         build(phase, 8, corner_spot)
-        run_class(8, corner_plan)
+        run_class(2, corner_plan)
 
     def own_rates(o, cx, cy, cz):
         rows = pl.ds(pl.multiple_of(o * SLOTS, SLOTS), SLOTS)
@@ -344,10 +366,13 @@
         accel = GRADIENT * (x * sums[0:1] - sums[1:4]) - gravity
         return accel, -GRADIENT * sums[4:5]
 
+    acc[...] = jnp.zeros_like(acc)
     filled = jnp.zeros((8, SLOTS), jnp.int32)
     for o in range(8):
         filled = jnp.where(row == o, occ_ref[o], filled)
     live = lane < filled
+    for load in loads:
+        load.wait()
     carried = jnp.where(live, mass_ref[...], 0.0)
     for which in (1, 2):
         chosen = jnp.logical_and(live, dir_ref[...] == which)
@@ -362,26 +387,39 @@
             0,
         )
 
+    slots = lax.broadcasted_iota(jnp.int32, (SLOTS, SLOTS), 0)
+    for which in range(2):
+        for o in range(8):
+            target = jnp.broadcast_to(code[which, o : o + 1, :], (SLOTS, SLOTS))
+            one_hot[which, :, o * SLOTS : (o + 1) * SLOTS] = jnp.where(slots == target, 1.0, 0.0).astype(BF16)
+    build_own(0)
     pl.semaphore_wait(barrier, greeted)
     start(0, x_faces + y_faces + z_faces)
     rates(0)
 
-    def to_half(o, carry):
+    def to_half(o):
         cx, cy, cz = 1 + o // 4, 1 + (o // 2) % 2, 1 + o % 2
         accel, rate = own_rates(o, cx, cy, cz)
         tile = first[cx, cy, cz]
         half[cx, cy, cz] = jnp.concatenate(
             [tile[3:6] + HALF_STEP * accel, tile[6:7] + HALF_STEP * rate], 0
         )
-        return carry
-
-    lax.fori_loop(0, 8, to_half, 0)
+
+    def over_own(update):
+        def four(at, carry):
+            for k in range(4):
+                update(4 * at + k)
+            return carry
+
+        lax.fori_loop(0, 2, four, 0)
+
+    over_own(to_half)
     start(1, x_faces + y_faces + z_faces)
+    acc[...] = jnp.zeros_like(acc)
+    build_own(1)
     rates(1)
 
-    slots = lax.broadcasted_iota(jnp.int32, (SLOTS, SLOTS), 0)
-
-    def to_new(o, found):
+    def to_new(o):
         cx, cy, cz = 1 + o // 4, 1 + (o // 2) % 2, 1 + o % 2
         accel, rate = own_rates(o, cx, cy, cz)
         tile = first[cx, cy, cz]
@@ -393,22 +431,18 @@
         fresh[o] = jnp.where(stays, new, 0.0)
         spot = jnp.where(row == 0, cx - 1, jnp.where(row == 1, cy - 1, jnp.where(row == 2, cz - 1, 0)))
         record = new + spot.astype(F32)
-        out = []
+        columns = pl.ds(pl.multiple_of(o * SLOTS, SLOTS), SLOTS)
         for which, by in ((0, -2.0), (1, 2.0)):
             parts = split3(record + jnp.where(row == 0, by, 0.0))
-            left = jnp.concatenate(parts, 0).astype(BF16)
-            target = jnp.broadcast_to(code[which, pl.ds(o, 1), :], (SLOTS, SLOTS))
-            chosen = jnp.where(slots == target, 1.0, 0.0).astype(BF16)
-            hit = lax.dot_general(
-                left, chosen, (((1,), (1,)), ((), ())), preferred_element_type=F32
-            )
-            out.append(found[which] + hit)
-        return tuple(out)
-
-    empty = jnp.zeros((24, SLOTS), F32)
-    found = lax.fori_loop(0, 8, to_new, (empty, empty))
+            stack = jnp.concatenate([*parts, jnp.zeros((8, SLOTS), F32)], 0)
+            records[which, :, columns] = stack.astype(BF16)
+
+    over_own(to_new)
     for which in range(2):
-        lists[which] = (found[which][0:8] + found[which][8:16]) + found[which][16:24]
+        found = lax.dot_general(
+            records[which], one_hot[which], (((1,), (1,)), ((), ())), preferred_element_type=F32
+        )
+        lists[which] = (found[0:8] + found[8:16]) + found[16:24]
 
     def list_copy(which):
         step = 1 if which == 0 else -1
@@ -459,6 +493,7 @@
 def body(offsets, velocity, density, mass, occupancy, move_direction, move_slot):
     vmem = pl.BlockSpec(memory_space=pltpu.VMEM)
     smem = pl.BlockSpec(memory_space=pltpu.SMEM)
+    hbm = pl.BlockSpec(memory_space=pl.ANY)
     pos, vel, rho, arr = pl.pallas_call(
         kernel,
         out_shape=(
@@ -467,9 +502,15 @@
             jax.ShapeDtypeStruct((8, SLOTS), F32),
             jax.ShapeDtypeStruct((14, SLOTS), F32),
         ),
-        in_specs=[vmem, vmem, vmem, vmem, smem, vmem, vmem],
+        in_specs=[hbm, hbm, hbm, hbm, smem, hbm, hbm],
         out_specs=(vmem, vmem, vmem, vmem),
         scratch_shapes=[
+            pltpu.VMEM((3, 8, SLOTS), F32),
+            pltpu.VMEM((3, 8, SLOTS), F32),
+            pltpu.VMEM((8, SLOTS), F32),
+            pltpu.VMEM((8, SLOTS), F32),
+            pltpu.VMEM((8, SLOTS), jnp.int32),
+            pltpu.VMEM((8, SLOTS), jnp.int32),
             pltpu.VMEM((4, 4, 4, 8, SLOTS), F32),
             pltpu.VMEM((4, 4, 4, 4, SLOTS), F32),
             pltpu.VMEM((64, 64, 2 * SLOTS), BF16),
@@ -483,13 +524,16 @@
             pltpu.VMEM((8, 8, SLOTS), F32),
             pltpu.VMEM((2, 8, SLOTS), F32),
             pltpu.VMEM((2, 8, SLOTS), F32),
+            pltpu.VMEM((2, 32, 8 * SLOTS), BF16),
+            pltpu.VMEM((2, SLOTS, 8 * SLOTS), BF16),
+            pltpu.SemaphoreType.DMA((6,)),
             pltpu.SemaphoreType.DMA((2, 26)),
             pltpu.SemaphoreType.DMA((2, 26)),
             pltpu.SemaphoreType.DMA((2,)),
             pltpu.SemaphoreType.DMA((2,)),
         ],
         compiler_params=pltpu.CompilerParams(
-            collective_id=0, has_side_effects=True, vmem_limit_bytes=48 << 20
+            collective_id=0, has_side_effects=True, vmem_limit_bytes=67_043_328
         ),
         name="sph_step",
     )(

time: 74.7 us -> 66.2 us (0.89)
  Pallas kernels: 66.5 us -> 60.5 us
  local copies, waits for them, and re-layouts: 6.62 us -> 4.54 us
    pallas_call x1, Pallas kernels: 66.5 us -> 60.5 us  [body(): pl.pallas_call(kernel, out_shape=(jax.ShapeDtypeStruct((3, 8, SLOTS), F32...]
    unnamed x15 -> x13, local copies, waits for them, and re-layouts: 5.25 us -> 3.35 us
where the time goes in v1:
time: 66.2 us; the launch traced here: 65.7 us
  Pallas kernels  60.5 us (91%)
  local copies, waits for them, and re-layouts  4.54 us (7%)
  between operations  0.67 us (1%)
    pallas_call x1, Pallas kernels, body(): pl.pallas_call(kernel, out_shape=(jax.ShapeDtypeStruct((3, 8, SLOTS), F32...  60.5 us
    unnamed x13, local copies, waits for them, and re-layouts  3.35 us

profile of v1, /device:TPU:1, one launch (start us, length us, event | category | flops | bytes accessed | tf_op | source)
XLA Modules:
  0.0 65.7 jit_solution(15193617308251847128)
XLA Ops:
  0.6 0.0 copy-start.4
  0.6 0.7 %copy-done.4 = s32[2,2,2]{2,1,0:T(2,128)S(1)} copy-done((s32[2,2,2]{2,1,0:T(2,128)S(1)}, s32[2,2,2]{2,1,0:T(2,128)}, u32[]{:S(2)}) %copy-start.4) | copy-done | bytes 56
  1.3 0.6 reshape.45.occ_ref
  1.9 60.5 %sph_step.1 = (f32[3,8,128]{2,1,0:T(8,128)}, f32[3,8,128]{2,1,0:T(8,128)}, f32[8,128]{1,0:T(8,128)}, f32[14,128]{1,0:T(8,128)}) custom-call(f32[3,8,128]{2,1,0:T(8,128)} %bitcast.12, f32[3,8,128]{2,1,0:T(8,128)} %bitcast.13, f32[8,128]{1,0:T(8,128)} %bitcast.16, f32[8,128]{1,0:T(8,128)} %bitcast.17, s32[8]{0:T(128)} %reshape.45.occ_ref, s32[8,128]{1,0:T(8,128)} %bitcast.18, ...), custom_call_target="tpu_custom_call" | custom-call | tf_op jit(solution)/shard_map/sph_step/pallas_call | solution.py:497
  62.4 0.0 copy-start.2
  62.4 0.0 copy-start.1
  62.5 0.7 %copy-done.2 = f32[14,128]{1,0:T(8,128)S(1)} copy-done((f32[14,128]{1,0:T(8,128)S(1)}, f32[14,128]{1,0:T(8,128)}, u32[]{:S(2)}) %copy-start.2) | copy-done | bytes 7192
  63.1 0.6 reshape.51
  63.7 0.0 copy-done.1
  63.7 0.0 copy-start
  63.7 0.6 copy.15
  64.3 0.1 copy-done
  64.5 0.0 copy-start.3
  64.5 0.6 copy.16
  65.1 0.1 copy-done.3
  65.1 0.6 copy.17
Async XLA Ops:
  0.6 0.7 %copy-start.4 = (s32[2,2,2]{2,1,0:T(2,128)S(1)}, s32[2,2,2]{2,1,0:T(2,128)}, u32[]{:S(2)}) copy-start(s32[2,2,2]{2,1,0:T(2,128)} %param.11) | copy-start | bytes 100
  62.4 0.7 %copy-start.2 = (f32[14,128]{1,0:T(8,128)S(1)}, f32[14,128]{1,0:T(8,128)}, u32[]{:S(2)}) copy-start(f32[14,128]{1,0:T(8,128)} %get-tuple-element.11) | copy-start | bytes 21508
  62.4 1.3 %copy-start.1 = (f32[3,8,128]{2,1,0:T(8,128)S(1)}, f32[3,8,128]{2,1,0:T(8,128)}, u32[]{:S(2)}) copy-start(f32[3,8,128]{2,1,0:T(8,128)} %get-tuple-element.8) | copy-start | bytes 36868
  63.7 0.7 %copy-start = (f32[3,8,128]{2,1,0:T(8,128)S(1)}, f32[3,8,128]{2,1,0:T(8,128)}, u32[]{:S(2)}) copy-start(f32[3,8,128]{2,1,0:T(8,128)} %get-tuple-element.9) | copy-start | bytes 36868
  64.5 0.7 %copy-start.3 = (f32[8,128]{1,0:T(8,128)S(1)}, f32[8,128]{1,0:T(8,128)}, u32[]{:S(2)}) copy-start(f32[8,128]{1,0:T(8,128)} %get-tuple-element.10) | copy-start | bytes 12292

commit v2 on v1

--- a/solution.py
+++ b/solution.py
@@ -46,9 +46,9 @@
 
 
 def kernel(
-    off_hbm, vel_hbm, rho_hbm, mass_hbm, occ_ref, dir_hbm, slot_hbm,
+    off_hbm, vel_hbm, rho_hbm, mass_hbm, occ_hbm, dir_hbm, slot_hbm,
     pos_out, vel_out, rho_out, arr_out,
-    off_ref, vel_ref, rho_ref, mass_ref, dir_ref, slot_ref,
+    off_ref, vel_ref, rho_ref, mass_ref, occ_ref, dir_ref, slot_ref,
     first, half, near_feat, own_feat, near_rows, own_q, own_t, geo, acc, code, fresh, lists, landed,
     records, one_hot, load_sem, send_sem, recv_sem, list_send, list_recv,
 ):
@@ -57,8 +57,8 @@
     row = row_iota()
     lane = lax.broadcasted_iota(jnp.int32, (8, SLOTS), 1)
 
-    sources = (off_hbm, vel_hbm, rho_hbm, mass_hbm, dir_hbm, slot_hbm)
-    held = (off_ref, vel_ref, rho_ref, mass_ref, dir_ref, slot_ref)
+    sources = (off_hbm, vel_hbm, rho_hbm, mass_hbm, occ_hbm, dir_hbm, slot_hbm)
+    held = (off_ref, vel_ref, rho_ref, mass_ref, occ_ref, dir_ref, slot_ref)
     loads = [
         pltpu.make_async_copy(source, target, load_sem.at[at])
         for at, (source, target) in enumerate(zip(sources, held))
@@ -173,57 +173,68 @@
             own_q[rows, :] = jnp.broadcast_to(stack[:, 56:57], (SLOTS, SLOTS))
             own_t[rows, :] = jnp.broadcast_to(stack[:, 57:58], (SLOTS, SLOTS))
 
-    def geometry(slot, groups):
-        at = 0
+    def products(slot, groups):
+        made, at = [], 0
         for owns, nears in groups:
-            left = own_feat[owns[0]]
-            if len(owns) > 1:
-                left = jnp.concatenate([own_feat[o] for o in owns], 0)
             for near in nears:
-                geo[slot, at, 0 : len(owns) * SLOTS, :] = jnp.dot(
-                    left, near_feat[near], preferred_element_type=F32
-                )
+
+                def make(owns=owns, near=near, at=at):
+                    left = own_feat[owns[0]]
+                    if len(owns) > 1:
+                        left = jnp.concatenate([own_feat[o] for o in owns], 0)
+                    geo[slot, at, 0 : len(owns) * SLOTS, :] = jnp.dot(
+                        left, near_feat[near], preferred_element_type=F32
+                    )
+
+                made.append(make)
                 at += 1
-
-    def pairs(slot, groups):
-        base = 0
+        return made
+
+    def add_pairs(slot, base, owns, nears, at, piece):
+        o = owns[at]
+        where = pl.ds(pl.multiple_of(o * SLOTS, SLOTS) + piece, CHUNK)
+        here = slice(at * SLOTS + piece, at * SLOTS + piece + CHUNK)
+        own_qs, own_ts = own_q[where, :], own_t[where, :]
+        sums = [acc[t, where, :] for t in range(5)]
+        for k, near in enumerate(nears):
+            x0, x1, x2, q, term, m = [near_rows[near, pl.ds(t, CHUNK, stride=0), :] for t in range(6)]
+            dist_sq = jnp.maximum(geo[slot, base + k, here, 0:SLOTS], TINY)
+            along = geo[slot, base + k, here, SLOTS : 2 * SLOTS]
+            fall = jnp.maximum(1.0 - dist_sq * lax.rsqrt(dist_sq), 0.0)
+            weight = fall * fall * fall * m
+            closing = jnp.minimum(along, 0.0) / ((dist_sq + EPS) * (own_qs + q))
+            push = weight * ((own_ts + term) - closing)
+            sums[0] = sums[0] + push
+            sums[1] = sums[1] + push * x0
+            sums[2] = sums[2] + push * x1
+            sums[3] = sums[3] + push * x2
+            sums[4] = sums[4] + weight * along
+        for t in range(5):
+            acc[t, where, :] = sums[t]
+
+    def both(ahead, ahead_groups, slot, groups):
+        made = products(ahead, ahead_groups)
+        units, base = [], 0
         for owns, nears in groups:
-            rows = []
-            for near in nears:
-                tile = near_rows[near]
-                rows.append([jnp.broadcast_to(tile[t : t + 1], (CHUNK, SLOTS)) for t in range(6)])
-            for at, o in enumerate(owns):
-                for piece in range(0, SLOTS, CHUNK):
-                    where = pl.ds(pl.multiple_of(o * SLOTS, SLOTS) + piece, CHUNK)
-                    here = slice(at * SLOTS + piece, at * SLOTS + piece + CHUNK)
-                    own_qs, own_ts = own_q[where, :], own_t[where, :]
-                    sums = [acc[t, where, :] for t in range(5)]
-                    for k in range(len(nears)):
-                        x0, x1, x2, q, term, m = rows[k]
-                        dist_sq = jnp.maximum(geo[slot, base + k, here, 0:SLOTS], TINY)
-                        along = geo[slot, base + k, here, SLOTS : 2 * SLOTS]
-                        fall = jnp.maximum(1.0 - dist_sq * lax.rsqrt(dist_sq), 0.0)
-                        weight = fall * fall * fall * m
-                        closing = jnp.minimum(along, 0.0) / ((dist_sq + EPS) * (own_qs + q))
-                        push = weight * ((own_ts + term) - closing)
-                        sums[0] = sums[0] + push
-                        sums[1] = sums[1] + push * x0
-                        sums[2] = sums[2] + push * x1
-                        sums[3] = sums[3] + push * x2
-                        sums[4] = sums[4] + weight * along
-                    for t in range(5):
-                        acc[t, where, :] = sums[t]
+            for at in range(len(owns)):
+                units += [(base, owns, nears, at, piece) for piece in range(0, SLOTS, CHUNK)]
             base += len(nears)
-
-    def run_class(steps, plan):
-        geometry(0, plan(0))
+        share = len(units) // len(made)
+        for at, make in enumerate(made):
+            make()
+            for base, owns, nears, which, piece in units[at * share : (at + 1) * share]:
+                add_pairs(slot, base, owns, nears, which, piece)
+
+    def run_class(steps, plan, hook=None):
+        for make in products(0, plan(0)):
+            make()
 
         def two(at, carry):
             step = 2 * at
-            geometry(1, plan(step + 1))
-            pairs(0, plan(step))
-            geometry(0, plan(jnp.minimum(step + 2, steps - 1)))
-            pairs(1, plan(step + 1))
+            if hook is not None:
+                hook(at)
+            both(1, plan(step + 1), 0, plan(step))
+            both(0, plan(jnp.minimum(step + 2, steps - 1)), 1, plan(step + 1))
             return carry
 
         lax.fori_loop(0, steps // 2, two, 0)
@@ -231,10 +242,10 @@
     def cell_at(cx, cy, cz):
         return cx * 16 + cy * 4 + cz
 
-    def own_plan(step):
+    def own_group(step):
         pair, side = step // 2, step % 2
         nears = [cell_at(1 + side, 1 + k // 2, 1 + k % 2) for k in range(4)]
-        return [([2 * pair, 2 * pair + 1], nears)]
+        return [2 * pair, 2 * pair + 1], nears
 
     def pick(axis, values):
         if isinstance(axis, int):
@@ -254,11 +265,14 @@
         ]
         return owns, nears
 
-    def yz_face_plan(step):
-        return [face_group(1 + step // 4, (step // 2) % 2, step % 2)]
-
-    def x_face_plan(step):
-        return [face_group(0, step // 2, step % 2)]
+    def main_plan(step):
+        face = step - 8
+        axis = jnp.where(step < 12, 1, jnp.where(step < 16, 2, 0))
+        inner = own_group(step)
+        outer = face_group(axis, (face // 2) % 2, face % 2)
+        return [
+            tuple([jnp.where(step < 8, i, o) for i, o in zip(a, b)] for a, b in zip(inner, outer))
+        ]
 
     def edge_plan(step):
         free, side = step // 2, step % 2
@@ -331,19 +345,27 @@
     corners = [r for r in REGIONS if r[0] and r[1] and r[2]]
 
     def rates(phase):
-        run_class(8, own_plan)
-        wait_in(phase, y_faces)
-        start(phase, yz_edges)
-        build(phase, 8, face_spot(1))
-        wait_in(phase, z_faces)
-        build(phase, 8, face_spot(2))
-        run_class(8, yz_face_plan)
-        wait_in(phase, x_faces)
-        start(phase, xy_edges + xz_edges)
-        build(phase, 8, face_spot(0))
-        run_class(4, x_face_plan)
-        wait_in(phase, xy_edges)
-        start(phase, corners)
+        def hook(at):
+            @pl.when(at == 3)
+            def _():
+                wait_in(phase, y_faces)
+                start(phase, yz_edges)
+                build(phase, 8, face_spot(1))
+                wait_in(phase, z_faces)
+                build(phase, 8, face_spot(2))
+
+            @pl.when(at == 7)
+            def _():
+                wait_in(phase, x_faces)
+                start(phase, xy_edges + xz_edges)
+                build(phase, 8, face_spot(0))
+
+            @pl.when(at == 9)
+            def _():
+                wait_in(phase, xy_edges)
+                start(phase, corners)
+
+        run_class(20, main_plan, hook)
         wait_in(phase, yz_edges)
         build(phase, 8, edge_spot(0))
         build(phase, 8, edge_spot(2))
@@ -367,12 +389,13 @@
         return accel, -GRADIENT * sums[4:5]
 
     acc[...] = jnp.zeros_like(acc)
-    filled = jnp.zeros((8, SLOTS), jnp.int32)
-    for o in range(8):
-        filled = jnp.where(row == o, occ_ref[o], filled)
-    live = lane < filled
     for load in loads:
         load.wait()
+    filled = []
+    for o in range(8):
+        y, z = (o // 2) % 2, o % 2
+        filled.append(jnp.broadcast_to(occ_ref[o // 4][y : y + 1, z : z + 1], (1, SLOTS)))
+    live = lane < jnp.concatenate(filled, 0)
     carried = jnp.where(live, mass_ref[...], 0.0)
     for which in (1, 2):
         chosen = jnp.logical_and(live, dir_ref[...] == which)
@@ -487,28 +510,37 @@
     for which in range(2):
         tile = landed[which]
         for k in range(7):
-            arr_out[2 * k + which : 2 * k + which + 1, :] = tile[k : k + 1]
+            arr_out[2 * k + which] = tile[k : k + 1]
+
+
+def hand_over(*refs):
+    given, results, sem = refs[:4], refs[4:8], refs[8]
+    copies = [pltpu.make_async_copy(a, b, sem.at[at]) for at, (a, b) in enumerate(zip(given, results))]
+    for copy in copies:
+        copy.start()
+    for copy in copies:
+        copy.wait()
 
 
 def body(offsets, velocity, density, mass, occupancy, move_direction, move_slot):
     vmem = pl.BlockSpec(memory_space=pltpu.VMEM)
-    smem = pl.BlockSpec(memory_space=pltpu.SMEM)
-    hbm = pl.BlockSpec(memory_space=pl.ANY)
+    hbm = pl.BlockSpec(memory_space=pltpu.HBM)
     pos, vel, rho, arr = pl.pallas_call(
         kernel,
         out_shape=(
             jax.ShapeDtypeStruct((3, 8, SLOTS), F32),
             jax.ShapeDtypeStruct((3, 8, SLOTS), F32),
             jax.ShapeDtypeStruct((8, SLOTS), F32),
-            jax.ShapeDtypeStruct((14, SLOTS), F32),
+            jax.ShapeDtypeStruct((14, 1, SLOTS), F32),
         ),
-        in_specs=[hbm, hbm, hbm, hbm, smem, hbm, hbm],
+        in_specs=[hbm] * 7,
         out_specs=(vmem, vmem, vmem, vmem),
         scratch_shapes=[
             pltpu.VMEM((3, 8, SLOTS), F32),
             pltpu.VMEM((3, 8, SLOTS), F32),
             pltpu.VMEM((8, SLOTS), F32),
             pltpu.VMEM((8, SLOTS), F32),
+            pltpu.VMEM((2, 2, 2), jnp.int32),
             pltpu.VMEM((8, SLOTS), jnp.int32),
             pltpu.VMEM((8, SLOTS), jnp.int32),
             pltpu.VMEM((4, 4, 4, 8, SLOTS), F32),
@@ -526,7 +558,7 @@
             pltpu.VMEM((2, 8, SLOTS), F32),
             pltpu.VMEM((2, 32, 8 * SLOTS), BF16),
             pltpu.VMEM((2, SLOTS, 8 * SLOTS), BF16),
-            pltpu.SemaphoreType.DMA((6,)),
+            pltpu.SemaphoreType.DMA((7,)),
             pltpu.SemaphoreType.DMA((2, 26)),
             pltpu.SemaphoreType.DMA((2, 26)),
             pltpu.SemaphoreType.DMA((2,)),
@@ -541,10 +573,18 @@
         velocity.reshape(3, 8, SLOTS),
         density.reshape(8, SLOTS),
         mass.reshape(8, SLOTS),
-        occupancy.reshape(8),
+        occupancy,
         move_direction.reshape(8, SLOTS),
         move_slot.reshape(8, SLOTS),
     )
+    pos, vel, rho, arr = pl.pallas_call(
+        hand_over,
+        out_shape=tuple(jax.ShapeDtypeStruct(a.shape, a.dtype) for a in (pos, vel, rho, arr)),
+        in_specs=[vmem] * 4,
+        out_specs=(pl.BlockSpec(memory_space=pltpu.HBM),) * 4,
+        scratch_shapes=[pltpu.SemaphoreType.DMA((4,))],
+        name="hand_over",
+    )(pos, vel, rho, arr)
     return (
         pos.reshape(offsets.shape),
         vel.reshape(velocity.shape),

time: 66.2 us -> 62.5 us (0.944)
  local copies, waits for them, and re-layouts: 4.54 us -> 0 us
  Pallas kernels: 60.5 us -> 61.5 us
    unnamed x13 -> x0, local copies, waits for them, and re-layouts: 3.35 us -> none
    pallas_call x0 -> x1, Pallas kernels: none -> 1.38 us  [body(): pl.pallas_call(hand_over, out_shape=tuple((jax.ShapeDtypeStruct(a.shape,...]
    reshape x2 -> x0, local copies, waits for them, and re-layouts: 1.19 us -> none  [the longest x1 0.6 us: body(): arr.reshape(7, 2, 1, 1, 1, SLOTS)]
where the time goes in v2:
time: 62.5 us; the launch traced here: 62.1 us
  Pallas kernels  61.5 us (98%)
  between operations  0.64 us (1%)
    pallas_call x1, Pallas kernels, body(): pl.pallas_call(kernel, out_shape=(jax.ShapeDtypeStruct((3, 8, SLOTS), F32...  60.1 us
    pallas_call x1, Pallas kernels, body(): pl.pallas_call(hand_over, out_shape=tuple((jax.ShapeDtypeStruct(a.shape,...  1.38 us

profile of v2, /device:TPU:1, one launch (start us, length us, event | category | flops | bytes accessed | tf_op | source)
XLA Modules:
  0.0 62.1 jit_solution(10167259788058059388)
XLA Ops:
  0.6 60.1 %sph_step.1 = (f32[3,8,128]{2,1,0:T(8,128)}, f32[3,8,128]{2,1,0:T(8,128)}, f32[8,128]{1,0:T(8,128)}, f32[14,1,128]{2,1,0:T(1,128)}) custom-call(f32[3,8,128]{2,1,0:T(8,128)} %bitcast.12, f32[3,8,128]{2,1,0:T(8,128)} %bitcast.13, f32[8,128]{1,0:T(8,128)} %bitcast.14, f32[8,128]{1,0:T(8,128)} %bitcast.15, s32[2,2,2]{2,1,0:T(2,128)} %occ_hbm.1, ...), custom_call_target="tpu_custom_call" | custom-call | tf_op jit(solution)/shard_map/sph_step/pallas_call | solution.py:528
  60.8 1.4 %hand_over.1 = (f32[3,8,128]{2,1,0:T(8,128)}, f32[3,8,128]{2,1,0:T(8,128)}, f32[8,128]{1,0:T(8,128)}, f32[14,1,128]{2,1,0:T(1,128)}) custom-call(f32[3,8,128]{2,1,0:T(8,128)} %get-tuple-element.12.refs_0_, f32[3,8,128]{2,1,0:T(8,128)} %get-tuple-element.13.refs_1_, f32[8,128]{1,0:T(8,128)} %get-tuple-element.14.refs_2_, f32[14,1,128]{2,1,0:T(1,128)} %get-tuple-element.15.refs_3_), custom_call_target="tpu_custom_call" | custom-call | tf_op jit(solution)/shard_map/hand_over/pallas_call | solution.py:580

commit v3 on v2

--- a/solution.py
+++ b/solution.py
@@ -329,12 +329,12 @@
 
     def build_own(phase):
         def two(at, carry):
-            for k in range(2):
-                o = 2 * at + k
+            for k in range(4):
+                o = 4 * at + k
                 features(phase, 1 + o // 4, 1 + (o // 2) % 2, 1 + o % 2, own=o)
             return carry
 
-        lax.fori_loop(0, 4, two, 0)
+        lax.fori_loop(0, 2, two, 0)
 
     x_faces = [(-1, 0, 0), (1, 0, 0)]
     y_faces = [(0, -1, 0), (0, 1, 0)]

time: 62.5 us -> 62.3 us (level)
  no operation moved by 1% of the time
where the time goes in v3:
time: 62.3 us; the launch traced here: 62 us
  Pallas kernels  61.3 us (98%)
  between operations  0.64 us (1%)
    pallas_call x1, Pallas kernels, body(): pl.pallas_call(kernel, out_shape=(jax.ShapeDtypeStruct((3, 8, SLOTS), F32...  60 us
    pallas_call x1, Pallas kernels, body(): pl.pallas_call(hand_over, out_shape=tuple((jax.ShapeDtypeStruct(a.shape,...  1.38 us

profile of v3, /device:TPU:1, one launch (start us, length us, event | category | flops | bytes accessed | tf_op | source)
XLA Modules:
  0.0 62.0 jit_solution(10407374350960033017)
XLA Ops:
  0.6 60.0 %sph_step.1 = (f32[3,8,128]{2,1,0:T(8,128)}, f32[3,8,128]{2,1,0:T(8,128)}, f32[8,128]{1,0:T(8,128)}, f32[14,1,128]{2,1,0:T(1,128)}) custom-call(f32[3,8,128]{2,1,0:T(8,128)} %bitcast.12, f32[3,8,128]{2,1,0:T(8,128)} %bitcast.13, f32[8,128]{1,0:T(8,128)} %bitcast.14, f32[8,128]{1,0:T(8,128)} %bitcast.15, s32[2,2,2]{2,1,0:T(2,128)} %occ_hbm.1, ...), custom_call_target="tpu_custom_call" | custom-call | tf_op jit(solution)/shard_map/sph_step/pallas_call | solution.py:528
  60.6 1.4 %hand_over.1 = (f32[3,8,128]{2,1,0:T(8,128)}, f32[3,8,128]{2,1,0:T(8,128)}, f32[8,128]{1,0:T(8,128)}, f32[14,1,128]{2,1,0:T(1,128)}) custom-call(f32[3,8,128]{2,1,0:T(8,128)} %get-tuple-element.12.refs_0_, f32[3,8,128]{2,1,0:T(8,128)} %get-tuple-element.13.refs_1_, f32[8,128]{1,0:T(8,128)} %get-tuple-element.14.refs_2_, f32[14,1,128]{2,1,0:T(1,128)} %get-tuple-element.15.refs_3_), custom_call_target="tpu_custom_call" | custom-call | tf_op jit(solution)/shard_map/hand_over/pallas_call | solution.py:580
